TPU v7x, 256 devices: a whole 4x4x8 slice. The times are simulated.
256 devices in a mesh: dp: 8 (over z), seq: 32 (over x, y, core).
Axes of the slice: x: 4, y: 4, z: 8, core: 2. Of those that a mesh axis runs over, the one named last changes fastest.
Arguments:
- seq_in: bfloat16 [65536, 1536], P(('dp', 'seq')), parts along dimension 0, may hold values from -6 to 6
- conv_gain: float32 [1536], replicated, may hold values from 0.1 to 1.9
- convolution_weight: bfloat16 [3, 1536, 768], replicated, may hold values from -0.09375 to 0.09375
- conv_bias: float32 [768], replicated, may hold values from -3 to 3
- attn_gain: float32 [1536], replicated, may hold values from 0.1 to 1.9
- w_query: bfloat16 [1536, 512], replicated
- w_key: bfloat16 [1536, 128], replicated
- w_value: bfloat16 [1536, 128], replicated, may hold values from -0.15625 to 0.15625
- w_out: bfloat16 [512, 1536], replicated, may hold values from -0.25 to 0.25
Outputs:
- block_out: bfloat16 [65536, 1536], P(('dp', 'seq')), parts along dimension 0
There are 8 independent parts, one for each index of `dp`. A program takes and returns all parts, laid end to end along the dimension named above; an argument that names none is the same for every part. Nothing has to cross between parts.
All inputs are finite; a program needn't handle non-finite values.
Results may differ from a plain program's by a relative error of at most 0.0059.
Values may be sent and summed in bfloat16 or wider, within the bound.
A program may use at most 128 MiB of HBM per device.

v0:
```python
import jax
import jax.numpy as jnp
from jax import lax
from jax.sharding import PartitionSpec as P

DILATION_STEP = 4


def padded(cells, sides, width):
    for axis, dim in sides:
        count = lax.axis_size(axis)
        ends = count - 1
        head = lax.slice_in_dim(cells, 0, width, axis=dim)
        tail = lax.slice_in_dim(cells, cells.shape[dim] - width, cells.shape[dim], axis=dim)
        cells = jnp.concatenate(
            [
                lax.ppermute(tail, axis, [(i, (i + 1) % count) for i in range(ends)]),
                cells,
                lax.ppermute(head, axis, [((i + 1) % count, i) for i in range(ends)]),
            ],
            axis=dim,
        )
    return cells


def normalize(values, gain_vec):
    wide = values.astype(jnp.float32)
    meansq = jnp.mean(wide * wide, axis=-1, keepdims=True)
    return wide * lax.rsqrt(meansq + 1e-06) * gain_vec


def fold_block(state_now, keys_vals, queries, head_dim):
    maxima, totals, summed = state_now
    key_part = keys_vals[:, :head_dim]
    value_part = keys_vals[:, head_dim:]
    scores = jnp.einsum(
        "thd,kd->htk", queries, key_part, preferred_element_type=jnp.float32
    ) * head_dim ** (-0.5)
    new_max = jnp.maximum(maxima, jnp.max(scores, axis=-1))
    factor = jnp.exp(maxima - new_max)
    expd = jnp.exp(scores - new_max[..., None])
    totals = totals * factor + jnp.sum(expd, axis=-1)
    summed = summed * factor[..., None] + jnp.einsum(
        "htk,kd->htd", expd.astype(jnp.bfloat16), value_part, preferred_element_type=jnp.float32
    )
    return (new_max, totals, summed)


def body(
    seq_in, conv_gain, convolution_weight, conv_bias, attn_gain, w_query, w_key, w_value, w_out
):
    token_rows = seq_in.shape[0]
    kernel_taps = convolution_weight.shape[0]
    head_dim = w_key.shape[1]
    heads_all = w_query.shape[1] // head_dim
    out_chan = convolution_weight.shape[2]
    receptive_reach = DILATION_STEP * (kernel_taps - 1) // 2
    normed = normalize(seq_in, conv_gain).astype(jnp.bfloat16)
    padded_tokens = padded(normed, (("seq", 0),), receptive_reach)
    convolved_total = jnp.dot(
        padded_tokens[0:token_rows], convolution_weight[0], preferred_element_type=jnp.float32
    )
    for tap_index in range(1, kernel_taps):
        convolved_total = convolved_total + jnp.dot(
            padded_tokens[tap_index * DILATION_STEP : tap_index * DILATION_STEP + token_rows],
            convolution_weight[tap_index],
            preferred_element_type=jnp.float32,
        )
    activated = jax.nn.gelu(convolved_total + conv_bias, approximate=True)
    wide_in = seq_in.astype(jnp.float32)
    hidden = jnp.concatenate(
        [wide_in[:, :out_chan] + activated, wide_in[:, out_chan:]], axis=1
    ).astype(jnp.bfloat16)
    attn_in = normalize(hidden, attn_gain).astype(jnp.bfloat16)
    queries = jnp.dot(attn_in, w_query, preferred_element_type=jnp.float32).astype(jnp.bfloat16)
    queries = queries.reshape(token_rows, heads_all, head_dim)
    key_rows = jnp.dot(attn_in, w_key, preferred_element_type=jnp.float32).astype(jnp.bfloat16)
    value_rows = jnp.dot(attn_in, w_value, preferred_element_type=jnp.float32).astype(jnp.bfloat16)
    packed = jnp.concatenate([key_rows, value_rows], axis=1)
    start_state = (
        jnp.full((heads_all, token_rows), -1e30, jnp.float32),
        jnp.zeros((heads_all, token_rows), jnp.float32),
        jnp.zeros((heads_all, token_rows, head_dim), jnp.float32),
    )
    gathered = lax.all_gather(packed, "seq", axis=0, tiled=True)
    shards = lax.axis_size("seq")
    group = 1
    for g in range(1, shards + 1):
        if shards % g == 0 and g * token_rows <= 2048:
            group = g
    span = token_rows * group
    count = gathered.shape[0] // span

    def step_keys(block_index, state_now):
        block_rows = lax.dynamic_slice_in_dim(gathered, block_index * span, span, 0)
        return fold_block(state_now, block_rows, queries, head_dim)

    final_state = lax.fori_loop(0, count, step_keys, start_state)
    maxima, totals, summed = final_state
    result = summed / totals[..., None]
    attended = (
        jnp.transpose(result, (1, 0, 2))
        .reshape(token_rows, heads_all * head_dim)
        .astype(jnp.bfloat16)
    )
    mixed = hidden.astype(jnp.float32) + jnp.dot(
        attended, w_out, preferred_element_type=jnp.float32
    )
    return mixed.astype(jnp.bfloat16)


def solution(mesh):
    placed = (P(("dp", "seq"), None), P(), P(), P(), P(), P(), P(), P(), P())
    return jax.shard_map(
        body, mesh=mesh, in_specs=placed, out_specs=P(("dp", "seq"), None), check_vma=False
    )
```

profile of v0, /device:TPU:1, one launch (start us, length us, event | category | flops | bytes accessed | tf_op | source)
XLA Modules:
  0.0 116.0 jit_solution(7414915342071189569)
XLA Ops:
  6.5 1.5 %multiply_reduce_fusion = f32[256]{0:T(256)S(1)} fusion(bf16[256,1536]{1,0:T(8,128)(2,1)} %param.11), kind=kLoop, calls=%fused_computation.34 | loop fusion | flops 1179392 | bytes 787456 | tf_op jit(solution)/shard_map/reduce_sum | solution.py:28
  8.0 1.4 %multiply_convert_fusion = bf16[256,1536]{1,0:T(8,128)(2,1)S(1)} fusion(f32[1536]{0:T(1024)} %param.12, f32[256]{0:T(256)S(1)} %add_rsqrt_fusion.1, bf16[256,1536]{1,0:T(8,128)(2,1)} %param.11), kind=kLoop, calls=%fused_computation.33 | loop fusion | flops 1572864 | bytes 1580032 | tf_op jit(solution)/shard_map/convert_element_type | solution.py:58
  9.5 4.6 %collective-permute-start = (bf16[4,1536]{1,0:T(4,128)(2,1)S(1)}, bf16[4,1536]{1,0:T(4,128)(2,1)S(1)}, u32[]{:S(2)}, u32[]{:S(2)}) collective-permute-start(bf16[4,1536]{1,0:T(4,128)(2,1)S(1)} %get-tuple-element.166), channel_id=1, source_target_pairs={{0,1},{1,2},{2,3},{3,4},{4,5},{5,6},{6,7},{7,8},{8,9},{9,10},{10,1... | collective-permute-start | bytes 36872 | tf_op jit(solution)/shard_map/ppermute | solution.py:17
  14.1 2.1 %collective-permute-start.1 = (bf16[4,1536]{1,0:T(4,128)(2,1)S(1)}, bf16[4,1536]{1,0:T(4,128)(2,1)S(1)}, u32[]{:S(2)}, u32[]{:S(2)}) collective-permute-start(bf16[4,1536]{1,0:T(4,128)(2,1)S(1)} %get-tuple-element.167), channel_id=1, source_target_pairs={{1,0},{2,1},{3,2},{4,3},{5,4},{6,5},{7,6},{8,7},{9,8},{10,9},{11,1... | collective-permute-start | bytes 36872 | tf_op jit(solution)/shard_map/ppermute | solution.py:19
  16.1 2.6 %fusion.15 = f32[256,768]{1,0:T(8,128)S(1)} fusion(bf16[256,1536]{1,0:T(8,128)(2,1)S(1)} %multiply_convert_fusion, bf16[3,1536,768]{2,1,0:T(8,128)(2,1)} %param.13), kind=kOutput, calls=%fused_computation.23 | convolution fusion | flops 603979776 | bytes 3932160 | tf_op jit(solution)/shard_map/dot_general | solution.py:64
  19.8 0.8 fusion.13
  20.7 1.0 fusion.47
  23.2 0.7 pad_maximum_fusion.5
  23.9 2.0 %fusion.34 = bf16[32,4,8,128]{3,2,1,0:T(8,128)(2,1)S(1)} fusion(bf16[1536,512]{1,0:T(8,128)(2,1)} %param.16, f32[1536]{0:T(1024)S(1)} %copy-done.5, f32[256]{0:T(256)S(1)} %add_rsqrt_fusion, bf16[256,768]{1,0:T(8,128)(2,1)S(1)} %slice.52, bf16[256,768]{1,0:T(8,128)(2,1)S(1)} %fusion.47), kind=kOutput, calls=%fused_computation.40 | convolution fusion | flops 405536768 | bytes 2628608 | tf_op jit(solution)/shard_map/dot_general | solution.py:75
  26.0 55.1 %all-gather.2.cloned.1.call-done = bf16[8192,256]{0,1:T(8,128)(2,1)} async-done(((bf16[256,256]{0,1:T(8,128)(2,1)}), bf16[8192,256]{0,1:T(8,128)(2,1)}) %all-gather.2.cloned.1.call-update) | async-done | bytes 4194320 | tf_op jit(solution)/shard_map/all_gather | solution.py:85
  81.1 26.3 %while.18 = (s32[]{:T(128)}, f32[4,256]{1,0:T(4,128)S(1)}, f32[4,256]{1,0:T(4,128)S(1)}, f32[4,256,128]{2,1,0:T(8,128)S(1)}, bf16[8192,256]{0,1:T(8,128)(2,1)}, ...) while((s32[]{:T(128)}, f32[4,256]{1,0:T(4,128)S(1)}, ...), condition=%wide.region_5.0_spmd.clone, body=%wide.region_2.0_spmd.clone.sunk | while | flops 1090917376 | bytes 27590852 | solution.py:98
  81.1 2.3 %bitcast_reduce_fusion.2 = (f32[4,256]{1,0:T(4,128)S(1)}, f32[2048,256,4]{1,0,2:T(8,128)S(1)}) fusion(bf16[256,4,128]{2,0,1:T(8,128)(2,1)S(1)} %get-tuple-element.240, bf16[8192,256]{0,1:T(8,128)(2,1)} %get-tuple-element.239, s32[]{:T(128)S(6)} %select_n.9), kind=kOutput, calls=%fused_computation.1.clone.1 | convolution fusion | flops 541064192 | bytes 9179140 | tf_op jit(solution)/shard_map/while/body/eval_jaxpr/thd,kd->htk/dot_general | solution.py:36
  83.4 1.4 %fusion.72 = f32[4,256]{1,0:T(4,128)S(1)} fusion(f32[2048,256,4]{1,0,2:T(8,128)S(1)} %get-tuple-element.210, f32[4,256]{1,0:T(4,128)S(1)} %select_maximum_fusion.2), kind=kLoop, calls=%fused_computation.4.clone.1 | loop fusion | flops 6290432 | bytes 8396800 | tf_op jit(solution)/shard_map/while/body/eval_jaxpr/reduce_sum | solution.py:42
  84.8 2.8 %fusion.74 = f32[4,256,128]{2,1,0:T(8,128)S(1)} fusion(f32[2048,256,4]{1,0,2:T(8,128)S(1)} %get-tuple-element.210, f32[4,256]{1,0:T(4,128)S(1)} %select_maximum_fusion.2, bf16[8192,256]{0,1:T(8,128)(2,1)} %get-tuple-element.239, s32[]{:T(128)S(6)} %select_n.9, s32[]{:T(128)S(6)} %add.170, f32[4,256,128]{2,1,0:T(8,128)S(1)} %get-tuple-element.227, ...), kind=kOutput, calls=%fused_computation.6.clone.1 | convolution fusion | flops 543555584 | bytes 9969673 | tf_op jit(solution)/shard_map/while/body/eval_jaxpr/htk,kd->htd/dot_general | solution.py:43
  87.7 2.4 %bitcast_reduce_fusion.2 = (f32[4,256]{1,0:T(4,128)S(1)}, f32[2048,256,4]{1,0,2:T(8,128)S(1)}) fusion(bf16[256,4,128]{2,0,1:T(8,128)(2,1)S(1)} %get-tuple-element.240, bf16[8192,256]{0,1:T(8,128)(2,1)} %get-tuple-element.239, s32[]{:T(128)S(6)} %select_n.9), kind=kOutput, calls=%fused_computation.1.clone.1 | convolution fusion | flops 541064192 | bytes 9179140 | tf_op jit(solution)/shard_map/while/body/eval_jaxpr/thd,kd->htk/dot_general | solution.py:36
  90.0 1.4 %fusion.72 = f32[4,256]{1,0:T(4,128)S(1)} fusion(f32[2048,256,4]{1,0,2:T(8,128)S(1)} %get-tuple-element.210, f32[4,256]{1,0:T(4,128)S(1)} %select_maximum_fusion.2), kind=kLoop, calls=%fused_computation.4.clone.1 | loop fusion | flops 6290432 | bytes 8396800 | tf_op jit(solution)/shard_map/while/body/eval_jaxpr/reduce_sum | solution.py:42
  91.4 2.8 %fusion.74 = f32[4,256,128]{2,1,0:T(8,128)S(1)} fusion(f32[2048,256,4]{1,0,2:T(8,128)S(1)} %get-tuple-element.210, f32[4,256]{1,0:T(4,128)S(1)} %select_maximum_fusion.2, bf16[8192,256]{0,1:T(8,128)(2,1)} %get-tuple-element.239, s32[]{:T(128)S(6)} %select_n.9, s32[]{:T(128)S(6)} %add.170, f32[4,256,128]{2,1,0:T(8,128)S(1)} %get-tuple-element.227, ...), kind=kOutput, calls=%fused_computation.6.clone.1 | convolution fusion | flops 543555584 | bytes 9969673 | tf_op jit(solution)/shard_map/while/body/eval_jaxpr/htk,kd->htd/dot_general | solution.py:43
  94.3 2.4 %bitcast_reduce_fusion.2 = (f32[4,256]{1,0:T(4,128)S(1)}, f32[2048,256,4]{1,0,2:T(8,128)S(1)}) fusion(bf16[256,4,128]{2,0,1:T(8,128)(2,1)S(1)} %get-tuple-element.240, bf16[8192,256]{0,1:T(8,128)(2,1)} %get-tuple-element.239, s32[]{:T(128)S(6)} %select_n.9), kind=kOutput, calls=%fused_computation.1.clone.1 | convolution fusion | flops 541064192 | bytes 9179140 | tf_op jit(solution)/shard_map/while/body/eval_jaxpr/thd,kd->htk/dot_general | solution.py:36
  96.6 1.4 %fusion.72 = f32[4,256]{1,0:T(4,128)S(1)} fusion(f32[2048,256,4]{1,0,2:T(8,128)S(1)} %get-tuple-element.210, f32[4,256]{1,0:T(4,128)S(1)} %select_maximum_fusion.2), kind=kLoop, calls=%fused_computation.4.clone.1 | loop fusion | flops 6290432 | bytes 8396800 | tf_op jit(solution)/shard_map/while/body/eval_jaxpr/reduce_sum | solution.py:42
  98.0 2.8 %fusion.74 = f32[4,256,128]{2,1,0:T(8,128)S(1)} fusion(f32[2048,256,4]{1,0,2:T(8,128)S(1)} %get-tuple-element.210, f32[4,256]{1,0:T(4,128)S(1)} %select_maximum_fusion.2, bf16[8192,256]{0,1:T(8,128)(2,1)} %get-tuple-element.239, s32[]{:T(128)S(6)} %select_n.9, s32[]{:T(128)S(6)} %add.170, f32[4,256,128]{2,1,0:T(8,128)S(1)} %get-tuple-element.227, ...), kind=kOutput, calls=%fused_computation.6.clone.1 | convolution fusion | flops 543555584 | bytes 9969673 | tf_op jit(solution)/shard_map/while/body/eval_jaxpr/htk,kd->htd/dot_general | solution.py:43
  100.8 2.4 %bitcast_reduce_fusion.2 = (f32[4,256]{1,0:T(4,128)S(1)}, f32[2048,256,4]{1,0,2:T(8,128)S(1)}) fusion(bf16[256,4,128]{2,0,1:T(8,128)(2,1)S(1)} %get-tuple-element.240, bf16[8192,256]{0,1:T(8,128)(2,1)} %get-tuple-element.239, s32[]{:T(128)S(6)} %select_n.9), kind=kOutput, calls=%fused_computation.1.clone.1 | convolution fusion | flops 541064192 | bytes 9179140 | tf_op jit(solution)/shard_map/while/body/eval_jaxpr/thd,kd->htk/dot_general | solution.py:36
  103.2 1.4 %fusion.72 = f32[4,256]{1,0:T(4,128)S(1)} fusion(f32[2048,256,4]{1,0,2:T(8,128)S(1)} %get-tuple-element.210, f32[4,256]{1,0:T(4,128)S(1)} %select_maximum_fusion.2), kind=kLoop, calls=%fused_computation.4.clone.1 | loop fusion | flops 6290432 | bytes 8396800 | tf_op jit(solution)/shard_map/while/body/eval_jaxpr/reduce_sum | solution.py:42
  104.6 2.8 %fusion.74 = f32[4,256,128]{2,1,0:T(8,128)S(1)} fusion(f32[2048,256,4]{1,0,2:T(8,128)S(1)} %get-tuple-element.210, f32[4,256]{1,0:T(4,128)S(1)} %select_maximum_fusion.2, bf16[8192,256]{0,1:T(8,128)(2,1)} %get-tuple-element.239, s32[]{:T(128)S(6)} %select_n.9, s32[]{:T(128)S(6)} %add.170, f32[4,256,128]{2,1,0:T(8,128)S(1)} %get-tuple-element.227, ...), kind=kOutput, calls=%fused_computation.6.clone.1 | convolution fusion | flops 543555584 | bytes 9969673 | tf_op jit(solution)/shard_map/while/body/eval_jaxpr/htk,kd->htd/dot_general | solution.py:43
  107.7 1.5 %fusion.12 = bf16[256,1536]{1,0:T(8,128)(2,1)} fusion(bf16[256,512]{0,1:T(8,128)(2,1)S(1)} %bitcast.71, bf16[512,1536]{1,0:T(8,128)(2,1)S(1)} %copy-done, bf16[256,768]{1,0:T(8,128)(2,1)S(1)} %slice.52, bf16[256,768]{1,0:T(8,128)(2,1)S(1)} %fusion.47), kind=kOutput, calls=%fused_computation.18 | convolution fusion | flops 405012480 | bytes 3407872 | tf_op jit(solution)/shard_map/dot_general | solution.py:106
  (44 shorter events, 3.0 us)
Async XLA Ops:
  6.5 101.2 %copy-start = (bf16[512,1536]{1,0:T(8,128)(2,1)S(1)}, bf16[512,1536]{1,0:T(8,128)(2,1)}, u32[]{:S(2)}) copy-start(bf16[512,1536]{1,0:T(8,128)(2,1)} %param.19) | copy-start | bytes 4718596
  6.5 74.5 %all-gather.2.cloned.1.call-start = ((), (), s32[]{:S(2)}) async-start(), calls=%async_computation | async-start | bytes 4325376 | tf_op jit(solution)/shard_map/all_gather | solution.py:85
  9.5 11.2 %collective-permute-start = (bf16[4,1536]{1,0:T(4,128)(2,1)S(1)}, bf16[4,1536]{1,0:T(4,128)(2,1)S(1)}, u32[]{:S(2)}, u32[]{:S(2)}) collective-permute-start(bf16[4,1536]{1,0:T(4,128)(2,1)S(1)} %get-tuple-element.166), channel_id=1, source_target_pairs={{0,1},{1,2},{2,3},{3,4},{4,5},{5,6},{6,7},{7,8},{8,9},{9,10},{10,1... | collective-permute-start | bytes 36872 | tf_op jit(solution)/shard_map/ppermute | solution.py:17
  14.1 4.7 %copy-start.1 = (bf16[256,1536]{1,0:T(8,128)(2,1)S(1)}, bf16[256,1536]{1,0:T(8,128)(2,1)}, u32[]{:S(2)}) copy-start(bf16[256,1536]{1,0:T(8,128)(2,1)} %param.11) | copy-start | bytes 2359300
  14.1 5.1 %collective-permute-start.1 = (bf16[4,1536]{1,0:T(4,128)(2,1)S(1)}, bf16[4,1536]{1,0:T(4,128)(2,1)S(1)}, u32[]{:S(2)}, u32[]{:S(2)}) collective-permute-start(bf16[4,1536]{1,0:T(4,128)(2,1)S(1)} %get-tuple-element.167), channel_id=1, source_target_pairs={{1,0},{2,1},{3,2},{4,3},{5,4},{6,5},{7,6},{8,7},{9,8},{10,9},{11,1... | collective-permute-start | bytes 36872 | tf_op jit(solution)/shard_map/ppermute | solution.py:19
  16.1 3.7 %copy-start.2 = (bf16[3,1536,768]{2,1,0:T(8,128)(2,1)S(1)}, bf16[3,1536,768]{2,1,0:T(8,128)(2,1)}, u32[]{:S(2)}) copy-start(bf16[3,1536,768]{2,1,0:T(8,128)(2,1)} %param.13) | copy-start | bytes 21233668
  19.0 1.7 %copy-start.6 = (f32[768]{0:T(1024)S(1)}, f32[768]{0:T(1024)}, u32[]{:S(2)}) copy-start(f32[768]{0:T(1024)} %param.14) | copy-start | bytes 9220
  20.6 1.3 %copy-start.3 = (bf16[1536,128]{1,0:T(8,128)(2,1)S(1)}, bf16[1536,128]{1,0:T(8,128)(2,1)}, u32[]{:S(2)}) copy-start(bf16[1536,128]{1,0:T(8,128)(2,1)} %param.18) | copy-start | bytes 1179652
  20.7 1.3 %copy-start.5 = (f32[1536]{0:T(1024)S(1)}, f32[1536]{0:T(1024)}, u32[]{:S(2)}) copy-start(f32[1536]{0:T(1024)} %param.15) | copy-start | bytes 18436
  21.7 1.0 copy-start.4
Sparse Core Ops, SparseCore 0:
  24.0 57.0 all-gather.1
where the time goes:
time: 117 us; the launch traced here: 116 us
  waiting for transfers between devices  55.3 us (47%)
  matrix products  29.4 us (25%)
  between operations  13.6 us (12%)
  other arithmetic  9.62 us (8%)
  starting transfers between devices  6.64 us (6%)
  local copies, waits for them, and re-layouts  1.19 us (1%)
    all_gather x1, waiting for transfers between devices, body(): gathered = lax.all_gather(packed, 'seq', axis=0, tiled=True)  55.1 us
    dot_general x4, matrix products, fold_block(): jnp.einsum('htk,kd->htd', expd.astype(jnp.bfloat16), value_part, preferre...  11.2 us
    dot_general x4, matrix products, fold_block(): jnp.einsum('thd,kd->htk', queries, key_part, preferred_element_type=jnp.f...  9.4 us
    reduce_sum x4, other arithmetic, fold_block(): totals = totals * factor + jnp.sum(expd, axis=-1)  5.49 us
    ppermute x1, starting transfers between devices, padded(): lax.ppermute(tail, axis, [(i, (i + 1) % count) for i in range(ends)])  4.58 us
    dot_general x2, matrix products, body(): jnp.dot(padded_tokens[tap_index * DILATION_STEP:tap_index * DILATION_STEP...  3.38 us
  transfers between devices with their start and end apart: 3, of which 2 were waited for; matrix products, arithmetic and copies ran while one was open for 5% of the time, Pallas kernels for 0%

commit v1 on v0

--- a/solution.py
+++ b/solution.py
@@ -82,7 +82,9 @@
         jnp.zeros((heads_all, token_rows), jnp.float32),
         jnp.zeros((heads_all, token_rows, head_dim), jnp.float32),
     )
-    gathered = lax.all_gather(packed, "seq", axis=0, tiled=True)
+    left_arr = jnp.stack([packed for _ in range(lax.axis_size("seq"))], axis=0)
+    current_arr = lax.all_to_all(left_arr, split_axis=0, axis_name="seq", concat_axis=0)
+    gathered = jnp.concatenate(current_arr, axis=0)
     shards = lax.axis_size("seq")
     group = 1
     for g in range(1, shards + 1):

time: 117 us -> 108 us (0.923)
  between operations: 13.6 us -> 0.27 us
  starting transfers between devices: 6.64 us -> 14.5 us
  waiting for transfers between devices: 55.3 us -> 50.2 us
  local copies, waits for them, and re-layouts: 1.19 us -> 3.75 us
    all_gather x1 -> x0, waiting for transfers between devices: 55.1 us -> none  [body(): gathered = lax.all_gather(packed, 'seq', axis=0, tiled=True)]
    all_to_all x0 -> x1, waiting for transfers between devices: none -> 50 us  [body(): lax.all_to_all(left_arr, split_axis=0, axis_name='seq', concat_axis=0)]
    all_to_all x0 -> x1, starting transfers between devices: none -> 7.83 us  [body(): lax.all_to_all(left_arr, split_axis=0, axis_name='seq', concat_axis=0)]
    another operation x0 -> x1, local copies, waits for them, and re-layouts: none -> 2.44 us  [body(): left_arr = jnp.stack([packed for _ in range(lax.axis_size('seq'))], axis=0)]
where the time goes in v1:
time: 108 us; the launch traced here: 107 us
  waiting for transfers between devices  50.2 us (46%)
  matrix products  29.1 us (27%)
  starting transfers between devices  14.5 us (13%)
  other arithmetic  8.97 us (8%)
  local copies, waits for them, and re-layouts  3.75 us (3%)
    all_to_all x1, waiting for transfers between devices, body(): lax.all_to_all(left_arr, split_axis=0, axis_name='seq', concat_axis=0)  50 us
    dot_general x4, matrix products, fold_block(): jnp.einsum('htk,kd->htd', expd.astype(jnp.bfloat16), value_part, preferre...  11.1 us
    dot_general x4, matrix products, fold_block(): jnp.einsum('thd,kd->htk', queries, key_part, preferred_element_type=jnp.f...  9.23 us
    all_to_all x1, starting transfers between devices, body(): lax.all_to_all(left_arr, split_axis=0, axis_name='seq', concat_axis=0)  7.83 us
    reduce_sum x4, other arithmetic, fold_block(): totals = totals * factor + jnp.sum(expd, axis=-1)  5.49 us
    ppermute x1, starting transfers between devices, padded(): lax.ppermute(tail, axis, [(i, (i + 1) % count) for i in range(ends)])  4.58 us
    dot_general x2, matrix products, body(): jnp.dot(padded_tokens[tap_index * DILATION_STEP:tap_index * DILATION_STEP...  3.39 us
    another operation x1, local copies, waits for them, and re-layouts, body(): left_arr = jnp.stack([packed for _ in range(lax.axis_size('seq'))], axis=0)  2.44 us
  transfers between devices with their start and end apart: 3, of which 2 were waited for; matrix products, arithmetic and copies ran while one was open for 5% of the time, Pallas kernels for 0%

profile of v1, /device:TPU:1, one launch (start us, length us, event | category | flops | bytes accessed | tf_op | source)
XLA Modules:
  0.0 107.0 jit_solution(13897760712812418780)
XLA Ops:
  0.0 1.5 %multiply_reduce_fusion = f32[256]{0:T(256)S(1)} fusion(bf16[256,1536]{1,0:T(8,128)(2,1)} %param.11), kind=kLoop, calls=%fused_computation.34 | loop fusion | flops 1179392 | bytes 787456 | tf_op jit(solution)/shard_map/reduce_sum | solution.py:28
  1.5 1.4 %multiply_convert_fusion = bf16[256,1536]{1,0:T(8,128)(2,1)S(1)} fusion(f32[1536]{0:T(1024)} %param.12, f32[256]{0:T(256)S(1)} %add_rsqrt_fusion.1, bf16[256,1536]{1,0:T(8,128)(2,1)} %param.11), kind=kLoop, calls=%fused_computation.33 | loop fusion | flops 1572864 | bytes 1580032 | tf_op jit(solution)/shard_map/convert_element_type | solution.py:58
  2.9 4.6 %collective-permute-start = (bf16[4,1536]{1,0:T(4,128)(2,1)S(1)}, bf16[4,1536]{1,0:T(4,128)(2,1)S(1)}, u32[]{:S(2)}, u32[]{:S(2)}) collective-permute-start(bf16[4,1536]{1,0:T(4,128)(2,1)S(1)} %get-tuple-element.166), channel_id=1, source_target_pairs={{0,1},{1,2},{2,3},{3,4},{4,5},{5,6},{6,7},{7,8},{8,9},{9,10},{10,1... | collective-permute-start | bytes 36872 | tf_op jit(solution)/shard_map/ppermute | solution.py:17
  7.5 2.1 %collective-permute-start.1 = (bf16[4,1536]{1,0:T(4,128)(2,1)S(1)}, bf16[4,1536]{1,0:T(4,128)(2,1)S(1)}, u32[]{:S(2)}, u32[]{:S(2)}) collective-permute-start(bf16[4,1536]{1,0:T(4,128)(2,1)S(1)} %get-tuple-element.167), channel_id=1, source_target_pairs={{1,0},{2,1},{3,2},{4,3},{5,4},{6,5},{7,6},{8,7},{9,8},{10,9},{11,1... | collective-permute-start | bytes 36872 | tf_op jit(solution)/shard_map/ppermute | solution.py:19
  9.6 2.6 %fusion.15 = f32[256,768]{1,0:T(8,128)S(1)} fusion(bf16[256,1536]{1,0:T(8,128)(2,1)S(1)} %multiply_convert_fusion, bf16[3,1536,768]{2,1,0:T(8,128)(2,1)} %param.13), kind=kOutput, calls=%fused_computation.23 | convolution fusion | flops 603979776 | bytes 3932160 | tf_op jit(solution)/shard_map/dot_general | solution.py:64
  14.2 1.0 fusion.47
  16.8 2.4 %stack.2 = bf16[32,256,256]{2,1,0:T(8,128)(2,1)} broadcast(bf16[256,256]{1,0:T(8,128)(2,1)S(1)} %copy.14), dimensions={1,2} | broadcast | bytes 4325376 | tf_op jit(solution)/shard_map/stack | solution.py:85
  19.2 7.8 %all-to-all-start = ((bf16[32,256,256]{2,1,0:T(8,128)(2,1)}), bf16[32,256,256]{2,1,0:T(8,128)(2,1)}, u32[]{:S(2)}, u32[]{:S(2)}) async-start(bf16[32,256,256]{2,1,0:T(8,128)(2,1)} %stack.2), calls=%async_computation | async-start | bytes 8388608 | tf_op jit(solution)/shard_map/all_to_all | solution.py:86
  27.1 2.0 %fusion.34 = bf16[32,4,8,128]{3,2,1,0:T(8,128)(2,1)S(1)} fusion(bf16[1536,512]{1,0:T(8,128)(2,1)} %param.16, f32[1536]{0:T(1024)S(1)} %copy-done.5, f32[256]{0:T(256)S(1)} %add_rsqrt_fusion, bf16[256,768]{1,0:T(8,128)(2,1)S(1)} %slice.52, bf16[256,768]{1,0:T(8,128)(2,1)S(1)} %fusion.47), kind=kOutput, calls=%fused_computation.40 | convolution fusion | flops 405536768 | bytes 2628608 | tf_op jit(solution)/shard_map/dot_general | solution.py:75
  29.2 50.0 %all-to-all-done = bf16[32,256,256]{2,1,0:T(8,128)(2,1)} async-done(((bf16[32,256,256]{2,1,0:T(8,128)(2,1)}), bf16[32,256,256]{2,1,0:T(8,128)(2,1)}, u32[]{:S(2)}, u32[]{:S(2)}) %all-to-all-start) | async-done | bytes 4194336 | tf_op jit(solution)/shard_map/all_to_all | solution.py:86
  79.2 26.0 %while.18 = (s32[]{:T(128)}, f32[4,256]{1,0:T(4,128)S(1)}, f32[4,256]{1,0:T(4,128)S(1)}, f32[4,256,128]{2,1,0:T(8,128)S(1)}, bf16[8192,256]{1,0:T(8,128)(2,1)}, ...) while((s32[]{:T(128)}, f32[4,256]{1,0:T(4,128)S(1)}, ...), condition=%wide.region_5.0_spmd.clone, body=%wide.region_2.0_spmd.clone.sunk | while | flops 1090917376 | bytes 27590852 | solution.py:100
  79.2 2.3 %bitcast_reduce_fusion.2 = (f32[4,256]{1,0:T(4,128)S(1)}, f32[2048,256,4]{1,0,2:T(8,128)S(1)}) fusion(bf16[256,4,128]{2,0,1:T(8,128)(2,1)S(1)} %get-tuple-element.240, bf16[8192,256]{1,0:T(8,128)(2,1)} %get-tuple-element.239, s32[]{:T(128)S(6)} %select_n.9), kind=kOutput, calls=%fused_computation.1.clone.1 | convolution fusion | flops 541064192 | bytes 9179140 | tf_op jit(solution)/shard_map/while/body/eval_jaxpr/thd,kd->htk/dot_general | solution.py:36
  81.5 1.4 %fusion.72 = f32[4,256]{1,0:T(4,128)S(1)} fusion(f32[2048,256,4]{1,0,2:T(8,128)S(1)} %get-tuple-element.210, f32[4,256]{1,0:T(4,128)S(1)} %select_maximum_fusion.2), kind=kLoop, calls=%fused_computation.4.clone.1 | loop fusion | flops 6290432 | bytes 8396800 | tf_op jit(solution)/shard_map/while/body/eval_jaxpr/reduce_sum | solution.py:42
  82.9 2.8 %fusion.74 = f32[4,256,128]{2,1,0:T(8,128)S(1)} fusion(f32[2048,256,4]{1,0,2:T(8,128)S(1)} %get-tuple-element.210, f32[4,256]{1,0:T(4,128)S(1)} %select_maximum_fusion.2, bf16[8192,256]{1,0:T(8,128)(2,1)} %get-tuple-element.239, s32[]{:T(128)S(6)} %select_n.9, s32[]{:T(128)S(6)} %add.170, f32[4,256,128]{2,1,0:T(8,128)S(1)} %get-tuple-element.227, ...), kind=kOutput, calls=%fused_computation.6.clone.1 | convolution fusion | flops 543555584 | bytes 9969673 | tf_op jit(solution)/shard_map/while/body/eval_jaxpr/htk,kd->htd/dot_general | solution.py:43
  85.7 2.3 %bitcast_reduce_fusion.2 = (f32[4,256]{1,0:T(4,128)S(1)}, f32[2048,256,4]{1,0,2:T(8,128)S(1)}) fusion(bf16[256,4,128]{2,0,1:T(8,128)(2,1)S(1)} %get-tuple-element.240, bf16[8192,256]{1,0:T(8,128)(2,1)} %get-tuple-element.239, s32[]{:T(128)S(6)} %select_n.9), kind=kOutput, calls=%fused_computation.1.clone.1 | convolution fusion | flops 541064192 | bytes 9179140 | tf_op jit(solution)/shard_map/while/body/eval_jaxpr/thd,kd->htk/dot_general | solution.py:36
  88.0 1.4 %fusion.72 = f32[4,256]{1,0:T(4,128)S(1)} fusion(f32[2048,256,4]{1,0,2:T(8,128)S(1)} %get-tuple-element.210, f32[4,256]{1,0:T(4,128)S(1)} %select_maximum_fusion.2), kind=kLoop, calls=%fused_computation.4.clone.1 | loop fusion | flops 6290432 | bytes 8396800 | tf_op jit(solution)/shard_map/while/body/eval_jaxpr/reduce_sum | solution.py:42
  89.4 2.8 %fusion.74 = f32[4,256,128]{2,1,0:T(8,128)S(1)} fusion(f32[2048,256,4]{1,0,2:T(8,128)S(1)} %get-tuple-element.210, f32[4,256]{1,0:T(4,128)S(1)} %select_maximum_fusion.2, bf16[8192,256]{1,0:T(8,128)(2,1)} %get-tuple-element.239, s32[]{:T(128)S(6)} %select_n.9, s32[]{:T(128)S(6)} %add.170, f32[4,256,128]{2,1,0:T(8,128)S(1)} %get-tuple-element.227, ...), kind=kOutput, calls=%fused_computation.6.clone.1 | convolution fusion | flops 543555584 | bytes 9969673 | tf_op jit(solution)/shard_map/while/body/eval_jaxpr/htk,kd->htd/dot_general | solution.py:43
  92.2 2.3 %bitcast_reduce_fusion.2 = (f32[4,256]{1,0:T(4,128)S(1)}, f32[2048,256,4]{1,0,2:T(8,128)S(1)}) fusion(bf16[256,4,128]{2,0,1:T(8,128)(2,1)S(1)} %get-tuple-element.240, bf16[8192,256]{1,0:T(8,128)(2,1)} %get-tuple-element.239, s32[]{:T(128)S(6)} %select_n.9), kind=kOutput, calls=%fused_computation.1.clone.1 | convolution fusion | flops 541064192 | bytes 9179140 | tf_op jit(solution)/shard_map/while/body/eval_jaxpr/thd,kd->htk/dot_general | solution.py:36
  94.5 1.4 %fusion.72 = f32[4,256]{1,0:T(4,128)S(1)} fusion(f32[2048,256,4]{1,0,2:T(8,128)S(1)} %get-tuple-element.210, f32[4,256]{1,0:T(4,128)S(1)} %select_maximum_fusion.2), kind=kLoop, calls=%fused_computation.4.clone.1 | loop fusion | flops 6290432 | bytes 8396800 | tf_op jit(solution)/shard_map/while/body/eval_jaxpr/reduce_sum | solution.py:42
  95.9 2.8 %fusion.74 = f32[4,256,128]{2,1,0:T(8,128)S(1)} fusion(f32[2048,256,4]{1,0,2:T(8,128)S(1)} %get-tuple-element.210, f32[4,256]{1,0:T(4,128)S(1)} %select_maximum_fusion.2, bf16[8192,256]{1,0:T(8,128)(2,1)} %get-tuple-element.239, s32[]{:T(128)S(6)} %select_n.9, s32[]{:T(128)S(6)} %add.170, f32[4,256,128]{2,1,0:T(8,128)S(1)} %get-tuple-element.227, ...), kind=kOutput, calls=%fused_computation.6.clone.1 | convolution fusion | flops 543555584 | bytes 9969673 | tf_op jit(solution)/shard_map/while/body/eval_jaxpr/htk,kd->htd/dot_general | solution.py:43
  98.7 2.3 %bitcast_reduce_fusion.2 = (f32[4,256]{1,0:T(4,128)S(1)}, f32[2048,256,4]{1,0,2:T(8,128)S(1)}) fusion(bf16[256,4,128]{2,0,1:T(8,128)(2,1)S(1)} %get-tuple-element.240, bf16[8192,256]{1,0:T(8,128)(2,1)} %get-tuple-element.239, s32[]{:T(128)S(6)} %select_n.9), kind=kOutput, calls=%fused_computation.1.clone.1 | convolution fusion | flops 541064192 | bytes 9179140 | tf_op jit(solution)/shard_map/while/body/eval_jaxpr/thd,kd->htk/dot_general | solution.py:36
  101.0 1.4 %fusion.72 = f32[4,256]{1,0:T(4,128)S(1)} fusion(f32[2048,256,4]{1,0,2:T(8,128)S(1)} %get-tuple-element.210, f32[4,256]{1,0:T(4,128)S(1)} %select_maximum_fusion.2), kind=kLoop, calls=%fused_computation.4.clone.1 | loop fusion | flops 6290432 | bytes 8396800 | tf_op jit(solution)/shard_map/while/body/eval_jaxpr/reduce_sum | solution.py:42
  102.4 2.8 %fusion.74 = f32[4,256,128]{2,1,0:T(8,128)S(1)} fusion(f32[2048,256,4]{1,0,2:T(8,128)S(1)} %get-tuple-element.210, f32[4,256]{1,0:T(4,128)S(1)} %select_maximum_fusion.2, bf16[8192,256]{1,0:T(8,128)(2,1)} %get-tuple-element.239, s32[]{:T(128)S(6)} %select_n.9, s32[]{:T(128)S(6)} %add.170, f32[4,256,128]{2,1,0:T(8,128)S(1)} %get-tuple-element.227, ...), kind=kOutput, calls=%fused_computation.6.clone.1 | convolution fusion | flops 543555584 | bytes 9969673 | tf_op jit(solution)/shard_map/while/body/eval_jaxpr/htk,kd->htd/dot_general | solution.py:43
  105.5 1.5 %fusion.12 = bf16[256,1536]{1,0:T(8,128)(2,1)} fusion(bf16[256,512]{0,1:T(8,128)(2,1)S(1)} %bitcast.70, bf16[512,1536]{1,0:T(8,128)(2,1)S(1)} %copy-done, bf16[256,768]{1,0:T(8,128)(2,1)S(1)} %slice.52, bf16[256,768]{1,0:T(8,128)(2,1)S(1)} %fusion.47), kind=kOutput, calls=%fused_computation.18 | convolution fusion | flops 405012480 | bytes 3407872 | tf_op jit(solution)/shard_map/dot_general | solution.py:108
  (45 shorter events, 3.9 us)
Async XLA Ops:
  0.0 105.5 %copy-start = (bf16[512,1536]{1,0:T(8,128)(2,1)S(1)}, bf16[512,1536]{1,0:T(8,128)(2,1)}, u32[]{:S(2)}) copy-start(bf16[512,1536]{1,0:T(8,128)(2,1)} %param.19) | copy-start | bytes 4718596
  2.9 11.2 %collective-permute-start = (bf16[4,1536]{1,0:T(4,128)(2,1)S(1)}, bf16[4,1536]{1,0:T(4,128)(2,1)S(1)}, u32[]{:S(2)}, u32[]{:S(2)}) collective-permute-start(bf16[4,1536]{1,0:T(4,128)(2,1)S(1)} %get-tuple-element.166), channel_id=1, source_target_pairs={{0,1},{1,2},{2,3},{3,4},{4,5},{5,6},{6,7},{7,8},{8,9},{9,10},{10,1... | collective-permute-start | bytes 36872 | tf_op jit(solution)/shard_map/ppermute | solution.py:17
  7.5 4.7 %copy-start.1 = (bf16[256,1536]{1,0:T(8,128)(2,1)S(1)}, bf16[256,1536]{1,0:T(8,128)(2,1)}, u32[]{:S(2)}) copy-start(bf16[256,1536]{1,0:T(8,128)(2,1)} %param.11) | copy-start | bytes 2359300
  7.5 5.1 %collective-permute-start.1 = (bf16[4,1536]{1,0:T(4,128)(2,1)S(1)}, bf16[4,1536]{1,0:T(4,128)(2,1)S(1)}, u32[]{:S(2)}, u32[]{:S(2)}) collective-permute-start(bf16[4,1536]{1,0:T(4,128)(2,1)S(1)} %get-tuple-element.167), channel_id=1, source_target_pairs={{1,0},{2,1},{3,2},{4,3},{5,4},{6,5},{7,6},{8,7},{9,8},{10,9},{11,1... | collective-permute-start | bytes 36872 | tf_op jit(solution)/shard_map/ppermute | solution.py:19
  9.6 3.7 %copy-start.2 = (bf16[3,1536,768]{2,1,0:T(8,128)(2,1)S(1)}, bf16[3,1536,768]{2,1,0:T(8,128)(2,1)}, u32[]{:S(2)}) copy-start(bf16[3,1536,768]{2,1,0:T(8,128)(2,1)} %param.13) | copy-start | bytes 21233668
  12.4 1.7 %copy-start.6 = (f32[768]{0:T(1024)S(1)}, f32[768]{0:T(1024)}, u32[]{:S(2)}) copy-start(f32[768]{0:T(1024)} %param.14) | copy-start | bytes 9220
  14.1 1.3 %copy-start.3 = (bf16[1536,128]{1,0:T(8,128)(2,1)S(1)}, bf16[1536,128]{1,0:T(8,128)(2,1)}, u32[]{:S(2)}) copy-start(bf16[1536,128]{1,0:T(8,128)(2,1)} %param.18) | copy-start | bytes 1179652
  14.1 1.3 %copy-start.5 = (f32[1536]{0:T(1024)S(1)}, f32[1536]{0:T(1024)}, u32[]{:S(2)}) copy-start(f32[1536]{0:T(1024)} %param.15) | copy-start | bytes 18436
  15.2 1.0 copy-start.4
  19.2 60.0 %all-to-all-start = ((bf16[32,256,256]{2,1,0:T(8,128)(2,1)}), bf16[32,256,256]{2,1,0:T(8,128)(2,1)}, u32[]{:S(2)}, u32[]{:S(2)}) async-start(bf16[32,256,256]{2,1,0:T(8,128)(2,1)} %stack.2), calls=%async_computation | async-start | bytes 8388608 | tf_op jit(solution)/shard_map/all_to_all | solution.py:86
